TPU v7x, 256 devices: a whole 4x4x8 slice. The times are simulated.
256 devices in a mesh: leaf: 32 (over z, x), batch: 8 (over y, core).
Axes of the slice: x: 4, y: 4, z: 8, core: 2. Of those that a mesh axis runs over, the one named last changes fastest.
Arguments:
- sources: bfloat16 [4096, 160, 1024], P('leaf', None, 'batch'), may hold values from -6 to 6
- mod_in: float32 [4096, 160], P('leaf'), may hold values from -1 to 1
- interp_in: bfloat16 [160, 64], replicated, may hold values from -0.5 to 0.5
- factors: bfloat16 [3, 4096, 64, 128], P(None, ('leaf', 'batch')), may hold values from -0.5 to 0.5
- interp_out: bfloat16 [160, 64], replicated, may hold values from -0.75 to 0.75
- mod_out: float32 [4096, 160], P('leaf'), may hold values from -1 to 1
Outputs:
- targets: bfloat16 [4096, 160, 1024], P('leaf', None, 'batch')
All inputs are finite; a program needn't handle non-finite values.
Results may differ from a plain program's by a relative error of at most 0.0076.
Values may be sent and summed in bfloat16 or wider, within the bound.
No kernel may reach another device: no remote copies, remote signals or barrier semaphores. Data moves between devices by JAX's collectives and lax.ppermute only.
A program may use at most 192 MiB of HBM per device.

v0:
```python
import jax
import jax.numpy as jnp
from jax import lax
from jax.sharding import PartitionSpec as P

LEVELS = 3


def partner_2(value, axis, distance):
    return lax.ppermute(value, axis, [(i, i ^ 1 << distance) for i in range(lax.axis_size(axis))])


def translate(weights, stacked):
    return jnp.einsum("brk,bkc->brc", weights, stacked, preferred_element_type=jnp.float32).astype(
        jnp.bfloat16
    )


def on_device(sources, mod_in, interp_in, factors, interp_out, mod_out):
    scaled = (mod_in[:, :, None] * sources.astype(jnp.float32)).astype(jnp.bfloat16)
    coeff = jnp.einsum("pr,bpc->brc", interp_in, scaled, preferred_element_type=jnp.float32).astype(
        jnp.bfloat16
    )
    for level in range(LEVELS):
        partner = partner_2(coeff, "leaf", level)
        stacked = jnp.concatenate([coeff, partner], axis=1)

        def apply_piece(piece, start, stacked=stacked):
            return translate(piece, stacked)

        coeff = apply_piece(
            lax.all_gather(factors[level], "batch", axis=0, tiled=True), jnp.int32(0)
        )
    values = jnp.einsum("qr,brc->bqc", interp_out, coeff, preferred_element_type=jnp.float32)
    return (values * mod_out[:, :, None]).astype(jnp.bfloat16)


def solution(mesh):
    return jax.shard_map(
        on_device,
        mesh=mesh,
        in_specs=(
            P("leaf", None, "batch"),
            P("leaf", None),
            P(),
            P(None, ("leaf", "batch"), None, None),
            P(),
            P("leaf", None),
        ),
        out_specs=P("leaf", None, "batch"),
        check_vma=False,
    )
```

profile of v0, /device:TPU:94, one launch (start us, length us, event | category | flops | bytes accessed | tf_op | source)
XLA Modules:
  0.0 180.1 jit_solution(12075313808552450980)
XLA Ops:
  6.5 0.0 copy-start
  6.5 0.0 all-gather.7.cloned.1.call-start
  6.5 2.0 %slice_bitcast_fusion = (bf16[1,16,64,128]{3,2,0,1:T(8,128)(2,1)}, bf16[1,16,64,128]{3,2,0,1:T(8,128)(2,1)}, bf16[1,16,64,128]{3,2,0,1:T(8,128)(2,1)}) fusion(bf16[3,16,64,128]{3,2,1,0:T(8,128)(2,1)} %param.9), kind=kLoop, calls=%fused_computation.25 | loop fusion | bytes 1572864
  8.6 0.0 all-gather.7.cloned.1.call-update
  8.6 0.0 all-gather.9.cloned.1.call-start
  8.6 0.7 all-gather.9.cloned.1.call-update
  9.3 0.0 all-gather.11.cloned.1.call-start
  9.4 1.0 copy.9
  10.4 5.6 %convert_bitcast_fusion.2 = bf16[128,64,128]{2,1,0:T(8,128)(2,1)S(1)} fusion(bf16[128,160,128]{2,1,0:T(8,128)(2,1)} %param.6, f32[128,160]{1,0:T(8,128)S(1)} %copy.9, bf16[160,64]{0,1:T(8,128)(2,1)} %param.8), kind=kOutput, calls=%fused_computation.24 | convolution fusion | flops 344457216 | bytes 7442432 | tf_op jit(solution)/shard_map/pr,bpc->brc/dot_general | solution.py:21
  16.0 0.9 collective-permute-start
  16.9 46.6 %collective-permute-done = bf16[128,64,128]{2,1,0:T(8,128)(2,1)} collective-permute-done((bf16[128,64,128]{2,1,0:T(8,128)(2,1)S(1)}, bf16[128,64,128]{2,1,0:T(8,128)(2,1)}, u32[]{:S(2)}, u32[]{:S(2)}) %collective-permute-start) | collective-permute-done | bytes 2097184 | tf_op jit(solution)/shard_map/ppermute | solution.py:10
  63.5 0.0 all-gather.7.cloned.1.call-done
  63.5 4.8 %convert_bitcast_fusion.1 = bf16[128,64,128]{2,1,0:T(8,128)(2,1)} fusion(bf16[128,64,128]{2,1,0:T(8,128)(2,1)} %collective-permute-done, bf16[128,64,128]{2,1,0:T(8,128)(2,1)S(1)} %convert_bitcast_fusion.2, bf16[1,128,64,128]{3,2,0,1:T(8,128)(2,1)} %all-gather.7.cloned.1.call-done), kind=kOutput, calls=%fused_computation.23 | convolution fusion | flops 277872640 | bytes 8388608 | tf_op jit(solution)/shard_map/brk,bkc->brc/dot_general | solution.py:14
  68.3 1.4 collective-permute-start.1
  69.8 0.0 all-gather.11.cloned.1.call-update
  69.8 0.0 copy-start.1
  69.8 0.0 all-gather.9.cloned.1.call-done
  69.8 46.8 %collective-permute-done.1 = bf16[128,64,128]{2,1,0:T(8,128)(2,1)S(1)} collective-permute-done((bf16[128,64,128]{2,1,0:T(8,128)(2,1)}, bf16[128,64,128]{2,1,0:T(8,128)(2,1)S(1)}, u32[]{:S(2)}, u32[]{:S(2)}) %collective-permute-start.1) | collective-permute-done | bytes 2097184 | tf_op jit(solution)/shard_map/ppermute | solution.py:10
  116.6 4.8 %convert_bitcast_fusion = bf16[128,64,128]{2,1,0:T(8,128)(2,1)} fusion(bf16[128,64,128]{2,1,0:T(8,128)(2,1)S(1)} %collective-permute-done.1, bf16[128,64,128]{2,1,0:T(8,128)(2,1)} %convert_bitcast_fusion.1, bf16[1,128,64,128]{3,2,0,1:T(8,128)(2,1)} %all-gather.9.cloned.1.call-done), kind=kOutput, calls=%fused_computation.22 | convolution fusion | flops 277872640 | bytes 8388608 | tf_op jit(solution)/shard_map/brk,bkc->brc/dot_general | solution.py:14
  121.4 2.0 %collective-permute-start.2 = (bf16[128,64,128]{2,1,0:T(8,128)(2,1)}, bf16[128,64,128]{2,1,0:T(8,128)(2,1)S(1)}, u32[]{:S(2)}, u32[]{:S(2)}) collective-permute-start(bf16[128,64,128]{2,1,0:T(8,128)(2,1)} %convert_bitcast_fusion), channel_id=1, source_target_pairs={{0,32},{8,40},{16,48},{24,56},{32,0},{40,8},{48,16},{56,24},{64,96... | collective-permute-start | bytes 6291464 | tf_op jit(solution)/shard_map/ppermute | solution.py:10
  123.3 0.0 copy-done.1
  123.3 0.1 copy.13
  123.4 0.0 all-gather.11.cloned.1.call-done
  123.4 44.0 %collective-permute-done.2 = bf16[128,64,128]{2,1,0:T(8,128)(2,1)S(1)} collective-permute-done((bf16[128,64,128]{2,1,0:T(8,128)(2,1)}, bf16[128,64,128]{2,1,0:T(8,128)(2,1)S(1)}, u32[]{:S(2)}, u32[]{:S(2)}) %collective-permute-start.2) | collective-permute-done | bytes 2097184 | tf_op jit(solution)/shard_map/ppermute | solution.py:10
  167.5 0.0 copy-done
  167.5 6.1 %fusion.1 = bf16[128,160,128]{2,1,0:T(8,128)(2,1)} fusion(f32[128,160]{1,0:T(8,128)S(1)} %copy.13, bf16[128,64,128]{2,1,0:T(8,128)(2,1)S(1)} %collective-permute-done.2, bf16[128,64,128]{2,1,0:T(8,128)(2,1)} %convert_bitcast_fusion, bf16[1,128,64,128]{3,2,0,1:T(8,128)(2,1)} %all-gather.11.cloned.1.call-done, bf16[160,64]{0,1:T(8,128)(2,1)S(1)} %copy-done), kind=kOutput, calls=%fused_computation.3 | convolution fusion | flops 618659840 | bytes 11636736 | tf_op jit(solution)/shard_map/qr,brc->bqc/dot_general | solution.py:34
Async XLA Ops:
  6.5 160.9 %copy-start = (bf16[160,64]{0,1:T(8,128)(2,1)S(1)}, bf16[160,64]{0,1:T(8,128)(2,1)}, u32[]{:S(2)}) copy-start(bf16[160,64]{0,1:T(8,128)(2,1)} %param.10) | copy-start | bytes 61444
  6.5 57.0 %all-gather.7.cloned.1.call-start = ((), (), s32[]{:S(2)}) async-start(), calls=%async_computation | async-start | bytes 2359296 | tf_op jit(solution)/shard_map/all_gather | solution.py:32
  8.6 61.2 %all-gather.9.cloned.1.call-start = ((), (), s32[]{:S(2)}) async-start(), calls=%async_computation.1 | async-start | bytes 2359296 | tf_op jit(solution)/shard_map/all_gather | solution.py:32
  9.3 114.1 %all-gather.11.cloned.1.call-start = ((), (), s32[]{:S(2)}) async-start(), calls=%async_computation.2 | async-start | bytes 2359296 | tf_op jit(solution)/shard_map/all_gather | solution.py:32
  16.0 47.6 %collective-permute-start = (bf16[128,64,128]{2,1,0:T(8,128)(2,1)S(1)}, bf16[128,64,128]{2,1,0:T(8,128)(2,1)}, u32[]{:S(2)}, u32[]{:S(2)}) collective-permute-start(bf16[128,64,128]{2,1,0:T(8,128)(2,1)S(1)} %convert_bitcast_fusion.2), channel_id=1, source_target_pairs={{0,8},{8,0},{16,24},{24,16},{32,40},{40,32},{48,56},{56,48},{64,72... | collective-permute-start | bytes 6291464 | tf_op jit(solution)/shard_map/ppermute | solution.py:10
  68.3 48.2 %collective-permute-start.1 = (bf16[128,64,128]{2,1,0:T(8,128)(2,1)}, bf16[128,64,128]{2,1,0:T(8,128)(2,1)S(1)}, u32[]{:S(2)}, u32[]{:S(2)}) collective-permute-start(bf16[128,64,128]{2,1,0:T(8,128)(2,1)} %convert_bitcast_fusion.1), channel_id=1, source_target_pairs={{0,16},{8,24},{16,0},{24,8},{32,48},{40,56},{48,32},{56,40},{64,80... | collective-permute-start | bytes 6291464 | tf_op jit(solution)/shard_map/ppermute | solution.py:10
  69.8 53.5 %copy-start.1 = (f32[128,160]{0,1:T(8,128)S(1)}, f32[128,160]{0,1:T(8,128)}, u32[]{:S(2)}) copy-start(f32[128,160]{0,1:T(8,128)} %param.11) | copy-start | bytes 245764
  121.4 46.1 %collective-permute-start.2 = (bf16[128,64,128]{2,1,0:T(8,128)(2,1)}, bf16[128,64,128]{2,1,0:T(8,128)(2,1)S(1)}, u32[]{:S(2)}, u32[]{:S(2)}) collective-permute-start(bf16[128,64,128]{2,1,0:T(8,128)(2,1)} %convert_bitcast_fusion), channel_id=1, source_target_pairs={{0,32},{8,40},{16,48},{24,56},{32,0},{40,8},{48,16},{56,24},{64,96... | collective-permute-start | bytes 6291464 | tf_op jit(solution)/shard_map/ppermute | solution.py:10
Sparse Core Ops, SparseCore 0:
  9.2 28.5 all-gather.6
  39.6 28.2 all-gather.8
  69.9 27.8 all-gather.10
where the time goes:
time: 180 us
  waiting for transfers between devices  138 us (77%)
  matrix products  21.3 us (12%)
  between operations  13.2 us (7%)
  starting transfers between devices  4.35 us (2%)
  local copies, waits for them, and re-layouts  3.1 us (2%)
    ppermute x3, waiting for transfers between devices, partner_2(): lax.ppermute(value, axis, [(i, i ^ 1 << distance) for i in range(lax.axis...  137 us
    dot_general x2, matrix products, translate(): jnp.einsum('brk,bkc->brc', weights, stacked, preferred_element_type=jnp.f...  9.59 us
    dot_general x1, matrix products, on_device(): jnp.einsum('qr,brc->bqc', interp_out, coeff, preferred_element_type=jnp.f...  6.11 us
    dot_general x1, matrix products, on_device(): jnp.einsum('pr,bpc->brc', interp_in, scaled, preferred_element_type=jnp.f...  5.6 us
    ppermute x3, starting transfers between devices, partner_2(): lax.ppermute(value, axis, [(i, i ^ 1 << distance) for i in range(lax.axis...  4.27 us
  transfers between devices with their start and end apart: 6, of which 3 were waited for; matrix products, arithmetic and copies ran while one was open for 9% of the time, Pallas kernels for 0%

commit v1 on v0

v1 whole, which is shorter than its diff:
```python
import jax
import jax.numpy as jnp
from jax import lax
from jax.experimental import pallas as pl
from jax.experimental.pallas import tpu as pltpu
from jax.sharding import PartitionSpec as P


LEVELS = 3
GROUP = 1 << LEVELS
AXES = ("leaf", "batch")
MIB = 1 << 20


SMEM = pl.BlockSpec(memory_space=pltpu.SMEM)
VMEM = pl.BlockSpec(memory_space=pltpu.VMEM)
HBM = pl.BlockSpec(memory_space=pltpu.HBM)

OUT_ORDER = ["o7", "o6", "o5", "o4", "o2", "o3", "o1"]


def exchange(value, node, batch):
    n_batch = lax.axis_size("batch")
    pairs = []
    for i in range(lax.axis_size("leaf")):
        for j in range(n_batch):
            pairs.append((i * n_batch + j, (i ^ node) * n_batch + (j ^ batch)))
    return lax.ppermute(value, AXES, pairs)


def interp_in_kernel(rs, index, sources, mod, weights, *refs):
    outs, (held, columns, rows, w, sems) = refs[: len(rs)], refs[len(rs) :]
    node, own = index[0], index[1]
    n_batch, _, per, _, _ = sources.shape
    small = [
        pltpu.make_async_copy(mod, columns, sems.at[len(rs)]),
        pltpu.make_async_copy(weights, w, sems.at[len(rs) + 1]),
    ]
    copies = []
    for at, r in enumerate(rs):
        copies.append(
            pltpu.make_async_copy(sources.at[:, node ^ r], held.at[at], sems.at[at])
        )
    for copy in small + copies:
        copy.start()
    for copy in small:
        copy.wait()
    rows[...] = columns[...].T
    wide = w[...].astype(jnp.float32)
    for at, r in enumerate(rs):
        copies[at].wait()
        for b in range(n_batch):
            for i in range(per):
                row = rows[pl.ds(b * GROUP * per + (node ^ r) * per + i, 1), :]
                outs[at][(own ^ b) * per + i] = jnp.dot(
                    (wide * row).astype(jnp.bfloat16),
                    held[at, b, i],
                    preferred_element_type=jnp.float32,
                ).astype(jnp.bfloat16)


def interp_in_call(rs, index, sources, mod, weights):
    n_batch, _, per, points, cols = sources.shape
    rank = weights.shape[0]

    def kernel(*refs):
        interp_in_kernel(rs, *refs)

    return pl.pallas_call(
        kernel,
        in_specs=[SMEM, HBM, HBM, HBM],
        out_specs=[VMEM] * len(rs),
        out_shape=[pltpu.VMEM((n_batch * per, rank, cols), jnp.bfloat16)] * len(rs),
        scratch_shapes=[
            pltpu.VMEM((len(rs), n_batch, per, points, cols), jnp.bfloat16),
            pltpu.VMEM(mod.shape, jnp.float32),
            pltpu.VMEM(mod.shape[::-1], jnp.float32),
            pltpu.VMEM(weights.shape, jnp.bfloat16),
            pltpu.SemaphoreType.DMA((len(rs) + 2,)),
        ],
        compiler_params=pltpu.CompilerParams(vmem_limit_bytes=8 * MIB),
        cost_estimate=pl.CostEstimate(
            flops=2 * len(rs) * n_batch * per * rank * points * cols,
            bytes_accessed=2 * len(rs) * n_batch * per * points * cols,
            transcendentals=0,
        ),
    )(index, sources, mod, weights)


def interp_out_kernel(r, index, coeff, mod, weights, *rest):
    out, held, sems = rest[-3:]
    node, own = index[0], index[1]
    n_batch, _, per, _, cols = out.shape
    boxes = n_batch * GROUP * per
    columns = pltpu.roll(mod[...], boxes - (node ^ r) * per, 1)
    w = weights[...]
    copies = []
    for b in range(n_batch):
        both = jnp.concatenate([coeff[(own ^ b) * per + i] for i in range(per)], axis=1)
        result = jnp.dot(w, both, preferred_element_type=jnp.float32)
        for i in range(per):
            j = b * GROUP * per + i
            held[b, i] = (result[:, i * cols : (i + 1) * cols] * columns[:, j : j + 1]).astype(
                jnp.bfloat16
            )
        copies.append(pltpu.make_async_copy(held.at[b], out.at[b, node ^ r], sems.at[b]))
        copies[-1].start()
    for copy in copies:
        copy.wait()


def interp_out_call(r, index, coeff, mod, weights, shape, running):
    n_batch, _, per, points, cols = shape
    in_specs = [SMEM, VMEM, VMEM, VMEM]
    operands = [index, coeff, mod, weights]
    aliases = {}
    if running is not None:
        in_specs.append(HBM)
        operands.append(running)
        aliases = {4: 0}

    def kernel(*refs):
        interp_out_kernel(r, *refs)

    return pl.pallas_call(
        kernel,
        in_specs=in_specs,
        out_specs=HBM,
        out_shape=jax.ShapeDtypeStruct(shape, jnp.bfloat16),
        scratch_shapes=[
            pltpu.VMEM((n_batch, per, points, cols), jnp.bfloat16),
            pltpu.SemaphoreType.DMA((n_batch,)),
        ],
        input_output_aliases=aliases,
        compiler_params=pltpu.CompilerParams(vmem_limit_bytes=8 * MIB),
        name="interp_out",
    )(*operands)


def levels_kernel(n_pieces, places, *refs):
    coeffs = refs[:GROUP]
    pieces = refs[GROUP : GROUP + n_pieces]
    outs = refs[GROUP + n_pieces :]
    _, _, per, rank, _ = pieces[0].shape
    for beta in sorted({place[0] for place in places}):
        source = {}
        for piece, (at, start, size) in zip(pieces, places):
            if at == beta:
                for r in range(size):
                    source[start + r] = (piece, r)
        state = [[coeffs[r][beta * per + i] for r in range(GROUP)] for i in range(per)]
        for level in range(LEVELS):
            bit = 1 << level
            after = [[None] * GROUP for _ in range(per)]
            for r in range(GROUP):
                q = r ^ bit
                if r > q:
                    continue
                for i in range(per):
                    fr = source[r][0][source[r][1], level, i]
                    fq = source[q][0][source[q][1], level, i]
                    fq = jnp.concatenate([fq[:, rank:], fq[:, :rank]], axis=1)
                    weights = jnp.concatenate([fr, fq], axis=0)
                    stacked = jnp.concatenate([state[i][r], state[i][q]], axis=0)
                    result = jnp.dot(
                        weights, stacked, preferred_element_type=jnp.float32
                    ).astype(jnp.bfloat16)
                    after[i][r], after[i][q] = result[:rank], result[rank:]
            state = after
        for i in range(per):
            for r in range(GROUP):
                outs[r][beta * per + i] = state[i][r]


def levels_call(coeffs, pieces, places):
    n_pieces = len(pieces)

    def kernel(*refs):
        levels_kernel(n_pieces, places, *refs)

    return pl.pallas_call(
        kernel,
        in_specs=[VMEM] * (GROUP + n_pieces),
        out_specs=[VMEM] * GROUP,
        out_shape=[pltpu.VMEM(c.shape, jnp.bfloat16) for c in coeffs],
        compiler_params=pltpu.CompilerParams(vmem_limit_bytes=16 * MIB),
        name="levels",
    )(*coeffs, *pieces)


def on_device(sources, mod_in, interp_in, factors, interp_out, mod_out):
    n_batch = lax.axis_size("batch")
    boxes, points, cols = sources.shape
    per = boxes // (n_batch * GROUP)
    node = lax.axis_index("leaf") & (GROUP - 1)
    index = jnp.stack([node, lax.axis_index("batch")]).astype(jnp.int32)

    held = []
    for r in range(GROUP):
        part = lax.dynamic_slice_in_dim(factors, (node ^ r) * per, per, axis=1)
        held.append(part if r == 0 else exchange(part, r, 0))
    mine = jnp.stack(held)
    half = GROUP // 2
    y1 = exchange(mine, 0, 2)
    y3 = exchange(mine, 0, 6)
    y2a = exchange(y1[:half], 0, 6)
    y2b = exchange(y3[half:], 0, 2)
    pieces, places = [], []
    for value, y, start, size in (
        (mine, 0, 0, GROUP),
        (y1, 1, 0, GROUP),
        (y3, 3, 0, GROUP),
        (y2a, 2, 0, half),
        (y2b, 2, half, half),
    ):
        pieces += [value, exchange(value, 0, 1)]
        places += [(2 * y, start, size), (2 * y + 1, start, size)]

    sources = sources.reshape(n_batch, GROUP, per, points, cols)
    sources = pltpu.with_memory_space_constraint(sources, pltpu.HBM)
    weights = pltpu.with_memory_space_constraint(interp_in.T, pltpu.HBM)
    mod = pltpu.with_memory_space_constraint(mod_in.T, pltpu.HBM)
    coeffs = [None] * GROUP
    for rs in ((7, 6, 5), (4, 2, 3, 1, 0)):
        parts = interp_in_call(rs, index, sources, mod, weights)
        for r, part in zip(rs, parts):
            coeffs[r] = part if r == 0 else exchange(part, r, 0)

    coeffs = levels_call(coeffs, pieces, places)

    out_points = interp_out.shape[0]
    out_view = (n_batch, GROUP, per, out_points, cols)
    mod = mod_out.T
    targets = None
    for name in ["o0"] + OUT_ORDER:
        r = int(name[1:])
        part = coeffs[r] if r == 0 else exchange(coeffs[r], r, 0)
        targets = interp_out_call(r, index, part, mod, interp_out, out_view, targets)
    return targets.reshape(boxes, out_points, cols)


def solution(mesh):
    return jax.shard_map(
        on_device,
        mesh=mesh,
        in_specs=(
            P("leaf", None, "batch"),
            P("leaf", None),
            P(),
            P(None, ("leaf", "batch"), None, None),
            P(),
            P("leaf", None),
        ),
        out_specs=P("leaf", None, "batch"),
        check_vma=False,
    )
```

time: 180 us -> 111 us (0.62)
  the two profiles are of different devices: /device:TPU:94 before, /device:TPU:1 now
where the time goes in v1:
time: 111 us
  starting transfers between devices  49.8 us (45%)
  waiting for transfers between devices  33.6 us (30%)
  Pallas kernels  24.6 us (22%)
  local copies, waits for them, and re-layouts  2.41 us (2%)
    ppermute x30, starting transfers between devices, exchange(): return lax.ppermute(value, AXES, pairs)  49.8 us
    ppermute x30, waiting for transfers between devices, exchange(): return lax.ppermute(value, AXES, pairs)  33.6 us
    pallas_call x8, Pallas kernels, interp_out_call(): pl.pallas_call(kernel, in_specs=in_specs, out_specs=HBM, out_shape=jax.Sh...  14.2 us
    pallas_call x2, Pallas kernels, interp_in_call(): pl.pallas_call(kernel, in_specs=[SMEM, HBM, HBM, HBM], out_specs=[VMEM] *...  6.17 us
    pallas_call x1, Pallas kernels, levels_call(): pl.pallas_call(kernel, in_specs=[VMEM] * (GROUP + n_pieces), out_specs=[V...  4.27 us
  transfers between devices with their start and end apart: 30, of which 11 were waited for; matrix products, arithmetic and copies ran while one was open for 1% of the time, Pallas kernels for 17%

profile of v1, /device:TPU:1, one launch (start us, length us, event | category | flops | bytes accessed | tf_op | source)
XLA Modules:
  0.0 110.9 jit_solution(8120174974833258846)
XLA Ops:
  0.0 1.2 %constant_dynamic-slice_fusion = (bf16[3,2,64,128]{3,2,1,0:T(8,128)(2,1)S(1)}, bf16[3,2,64,128]{3,2,1,0:T(8,128)(2,1)S(1)}, bf16[3,2,64,128]{3,2,1,0:T(8,128)(2,...) fusion(bf16[3,16,64,128]{3,2,1,0:T(8,128)(2,1)} %param.9, ...), kind=kLoop, calls=%fused_computation.8 | loop fusion | bytes 1376284 | tf_op jit(solution)/shard_map/dynamic_slice | solution.py:200
  1.2 4.7 %collective-permute-start.13 = (bf16[3,2,64,128]{3,2,1,0:T(8,128)(2,1)S(1)}, bf16[3,2,64,128]{3,2,1,0:T(8,128)(2,1)S(1)}, u32[]{:S(2)}, u32[]{:S(2)}) collective-permute-start(bf16[3,2,64,128]{3,2,1,0:T(8,128)(2,1)S(1)} %get-tuple-element.37), channel_id=1, source_target_pairs={{0,56},{1,57},{2,58},{3,59},{4,60},{5,61},{6,62},{7,63},{8,48},{9,... | collective-permute-start | bytes 294920 | tf_op jit(solution)/shard_map/ppermute | solution.py:28
  6.0 1.1 %collective-permute-start.10 = (bf16[3,2,64,128]{3,2,1,0:T(8,128)(2,1)S(1)}, bf16[3,2,64,128]{3,2,1,0:T(8,128)(2,1)S(1)}, u32[]{:S(2)}, u32[]{:S(2)}) collective-permute-start(bf16[3,2,64,128]{3,2,1,0:T(8,128)(2,1)S(1)} %get-tuple-element.39), channel_id=1, source_target_pairs={{0,32},{1,33},{2,34},{3,35},{4,36},{5,37},{6,38},{7,39},{8,40},{9,... | collective-permute-start | bytes 294920 | tf_op jit(solution)/shard_map/ppermute | solution.py:28
  7.1 0.9 collective-permute-start.9
  8.0 0.7 collective-permute-start.7
  8.6 0.9 bitcast_dynamic-update-slice_fusion.7
  9.5 2.9 %collective-permute-done.7 = bf16[3,2,64,128]{3,2,1,0:T(8,128)(2,1)S(1)} collective-permute-done((bf16[3,2,64,128]{3,2,1,0:T(8,128)(2,1)S(1)}, bf16[3,2,64,128]{3,2,1,0:T(8,128)(2,1)S(1)}, u32[]{:S(2)}, u32[]{:S(2)}) %collective-permute-start.7) | collective-permute-done | bytes 98336 | tf_op jit(solution)/shard_map/ppermute | solution.py:28
  12.4 2.5 %collective-permute-start.8 = (bf16[3,2,64,128]{3,2,1,0:T(8,128)(2,1)S(1)}, bf16[3,2,64,128]{3,2,1,0:T(8,128)(2,1)S(1)}, u32[]{:S(2)}, u32[]{:S(2)}) collective-permute-start(bf16[3,2,64,128]{3,2,1,0:T(8,128)(2,1)S(1)} %get-tuple-element.41), channel_id=1, source_target_pairs={{0,16},{1,17},{2,18},{3,19},{4,20},{5,21},{6,22},{7,23},{8,24},{9,... | collective-permute-start | bytes 294920 | tf_op jit(solution)/shard_map/ppermute | solution.py:28
  14.9 2.5 %collective-permute-done.8 = bf16[3,2,64,128]{3,2,1,0:T(8,128)(2,1)S(1)} collective-permute-done((bf16[3,2,64,128]{3,2,1,0:T(8,128)(2,1)S(1)}, bf16[3,2,64,128]{3,2,1,0:T(8,128)(2,1)S(1)}, u32[]{:S(2)}, u32[]{:S(2)}) %collective-permute-start.8) | collective-permute-done | bytes 98336 | tf_op jit(solution)/shard_map/ppermute | solution.py:28
  17.4 2.5 %collective-permute-start.12 = (bf16[3,2,64,128]{3,2,1,0:T(8,128)(2,1)S(1)}, bf16[3,2,64,128]{3,2,1,0:T(8,128)(2,1)S(1)}, u32[]{:S(2)}, u32[]{:S(2)}) collective-permute-start(bf16[3,2,64,128]{3,2,1,0:T(8,128)(2,1)S(1)} %get-tuple-element.43), channel_id=1, source_target_pairs={{0,48},{1,49},{2,50},{3,51},{4,52},{5,53},{6,54},{7,55},{8,56},{9,... | collective-permute-start | bytes 294920 | tf_op jit(solution)/shard_map/ppermute | solution.py:28
  20.0 3.3 %collective-permute-done.12 = bf16[3,2,64,128]{3,2,1,0:T(8,128)(2,1)S(1)} collective-permute-done((bf16[3,2,64,128]{3,2,1,0:T(8,128)(2,1)S(1)}, bf16[3,2,64,128]{3,2,1,0:T(8,128)(2,1)S(1)}, u32[]{:S(2)}, u32[]{:S(2)}) %collective-permute-start.12) | collective-permute-done | bytes 98336 | tf_op jit(solution)/shard_map/ppermute | solution.py:28
  23.3 2.8 %collective-permute-start.17 = (bf16[8,3,2,64,128]{4,3,2,1,0:T(8,128)(2,1)S(1)}, bf16[8,3,2,64,128]{4,3,2,1,0:T(8,128)(2,1)S(1)}, u32[]{:S(2)}, u32[]{:S(2)}) collective-permute-start(bf16[8,3,2,64,128]{4,3,2,1,0:T(8,128)(2,1)S(1)} %bitcast_dynamic-update-slice_fusion.refs_8_), channel_id=1, source_target_pairs={{0,6},{1,7},{2,4},{3,5},{4,2},{5,3},{6,0},{7,1},{8,14},{9,15},{10,... | collective-permute-start | bytes 2359304 | tf_op jit(solution)/shard_map/ppermute | solution.py:28
  26.2 2.7 %shard_map.65 = (bf16[16,64,128]{2,1,0:T(8,128)(2,1)S(1)}, bf16[16,64,128]{2,1,0:T(8,128)(2,1)S(1)}, bf16[16,64,128]{2,1,0:T(8,128)(2,1)S(1)}) custom-call(s32[2]{0:T(128)S(1)} %pad_add_fusion.refs_0_, bf16[8,8,2,160,128]{4,3,2,1,0:T(8,128)(2,1)} %bitcast.31, f32[160,128]{1,0:T(8,128)} %bitcast.33, bf16[64,160]{1,0:T(8,128)(2,1)} %bitcast.35), custom_call_target="tpu_custom_call" | custom-call | flops 125829120 | bytes 1966080 | tf_op jit(solution)/shard_map/pallas_call | solution.py:69
  29.0 0.8 collective-permute-start.4
  29.8 2.9 %collective-permute-start.5 = (bf16[16,64,128]{2,1,0:T(8,128)(2,1)S(1)}, bf16[16,64,128]{2,1,0:T(8,128)(2,1)S(1)}, u32[]{:S(2)}, u32[]{:S(2)}) collective-permute-start(bf16[16,64,128]{2,1,0:T(8,128)(2,1)S(1)} %get-tuple-element.27), channel_id=1, source_target_pairs={{0,48},{1,49},{2,50},{3,51},{4,52},{5,53},{6,54},{7,55},{8,56},{9,... | collective-permute-start | bytes 786440 | tf_op jit(solution)/shard_map/ppermute | solution.py:28
  32.7 1.2 %collective-permute-start.6 = (bf16[16,64,128]{2,1,0:T(8,128)(2,1)S(1)}, bf16[16,64,128]{2,1,0:T(8,128)(2,1)S(1)}, u32[]{:S(2)}, u32[]{:S(2)}) collective-permute-start(bf16[16,64,128]{2,1,0:T(8,128)(2,1)S(1)} %get-tuple-element.28), channel_id=1, source_target_pairs={{0,56},{1,57},{2,58},{3,59},{4,60},{5,61},{6,62},{7,63},{8,48},{9,... | collective-permute-start | bytes 786440 | tf_op jit(solution)/shard_map/ppermute | solution.py:28
  33.9 3.4 %shard_map.64 = (bf16[16,64,128]{2,1,0:T(8,128)(2,1)S(1)}, bf16[16,64,128]{2,1,0:T(8,128)(2,1)S(1)}, bf16[16,64,128]{2,1,0:T(8,128)(2,1)S(1)}, bf16[16,64,128]{2,1,0:T(8,128)(2,1)S(1)}, bf16[16,64,128]{2,1,0:T(8,128)(2,1)S(1)}) custom-call(s32[2]{0:T(128)S(1)} %pad_add_fusion.refs_0_, bf16[8,8,2,160,128]{4,3,2,1,0:T(8,128)(2,1)} %bitcast.32, ...), custom_call_target="tpu_custom_call" | custom-call | flops 209715200 | bytes 3276800 | tf_op jit(solution)/shard_map/pallas_call | solution.py:69
  37.4 2.1 %collective-permute-done.5.refs_6_ = bf16[16,64,128]{2,1,0:T(8,128)(2,1)S(1)} collective-permute-done((bf16[16,64,128]{2,1,0:T(8,128)(2,1)S(1)}, bf16[16,64,128]{2,1,0:T(8,128)(2,1)S(1)}, u32[]{:S(2)}, u32[]{:S(2)}) %collective-permute-start.5) | collective-permute-done | bytes 262176 | tf_op jit(solution)/shard_map/ppermute | solution.py:28
  39.6 2.6 %collective-permute-start.1 = (bf16[16,64,128]{2,1,0:T(8,128)(2,1)S(1)}, bf16[16,64,128]{2,1,0:T(8,128)(2,1)S(1)}, u32[]{:S(2)}, u32[]{:S(2)}) collective-permute-start(bf16[16,64,128]{2,1,0:T(8,128)(2,1)S(1)} %get-tuple-element.23), channel_id=1, source_target_pairs={{0,16},{1,17},{2,18},{3,19},{4,20},{5,21},{6,22},{7,23},{8,24},{9,... | collective-permute-start | bytes 786440 | tf_op jit(solution)/shard_map/ppermute | solution.py:28
  42.2 1.3 %collective-permute-start.3 = (bf16[16,64,128]{2,1,0:T(8,128)(2,1)S(1)}, bf16[16,64,128]{2,1,0:T(8,128)(2,1)S(1)}, u32[]{:S(2)}, u32[]{:S(2)}) collective-permute-start(bf16[16,64,128]{2,1,0:T(8,128)(2,1)S(1)} %get-tuple-element.25), channel_id=1, source_target_pairs={{0,32},{1,33},{2,34},{3,35},{4,36},{5,37},{6,38},{7,39},{8,40},{9,... | collective-permute-start | bytes 786440 | tf_op jit(solution)/shard_map/ppermute | solution.py:28
  43.5 0.9 collective-permute-done.6.refs_7_
  44.4 10.0 %collective-permute-start.14 = (bf16[8,3,2,64,128]{4,3,2,1,0:T(8,128)(2,1)S(1)}, bf16[8,3,2,64,128]{4,3,2,1,0:T(8,128)(2,1)S(1)}, u32[]{:S(2)}, u32[]{:S(2)}) collective-permute-start(bf16[8,3,2,64,128]{4,3,2,1,0:T(8,128)(2,1)S(1)} %bitcast_dynamic-update-slice_fusion.refs_8_), channel_id=1, source_target_pairs={{0,1},{1,0},{2,3},{3,2},{4,5},{5,4},{6,7},{7,6},{8,9},{9,8},{10,11... | collective-permute-start | bytes 2359304 | tf_op jit(solution)/shard_map/ppermute | solution.py:28
  54.4 1.8 %collective-permute-start.21 = (bf16[4,3,2,64,128]{4,3,2,1,0:T(8,128)(2,1)S(1)}, bf16[4,3,2,64,128]{4,3,2,1,0:T(8,128)(2,1)S(1)}, u32[]{:S(2)}, u32[]{:S(2)}) collective-permute-start(bf16[4,3,2,64,128]{4,3,2,1,0:T(8,128)(2,1)S(1)} %slice.9), channel_id=1, source_target_pairs={{0,2},{1,3},{2,0},{3,1},{4,6},{5,7},{6,4},{7,5},{8,10},{9,11},{10,... | collective-permute-start | bytes 1179656 | tf_op jit(solution)/shard_map/ppermute | solution.py:28
  56.2 3.7 %collective-permute-done.2.refs_3_ = bf16[16,64,128]{2,1,0:T(8,128)(2,1)S(1)} collective-permute-done((bf16[16,64,128]{2,1,0:T(8,128)(2,1)S(1)}, bf16[16,64,128]{2,1,0:T(8,128)(2,1)S(1)}, u32[]{:S(2)}, u32[]{:S(2)}) %collective-permute-start.2) | collective-permute-done | bytes 262176 | tf_op jit(solution)/shard_map/ppermute | solution.py:28
  59.9 2.6 %collective-permute-start.18 = (bf16[8,3,2,64,128]{4,3,2,1,0:T(8,128)(2,1)S(1)}, bf16[8,3,2,64,128]{4,3,2,1,0:T(8,128)(2,1)S(1)}, u32[]{:S(2)}, u32[]{:S(2)}) collective-permute-start(bf16[8,3,2,64,128]{4,3,2,1,0:T(8,128)(2,1)S(1)} %collective-permute-done.17.refs_12_), channel_id=1, source_target_pairs={{0,1},{1,0},{2,3},{3,2},{4,5},{5,4},{6,7},{7,6},{8,9},{9,8},{10,11... | collective-permute-start | bytes 2359304 | tf_op jit(solution)/shard_map/ppermute | solution.py:28
  62.5 3.2 %collective-permute-done.21.refs_16_ = bf16[4,3,2,64,128]{4,3,2,1,0:T(8,128)(2,1)S(1)} collective-permute-done((bf16[4,3,2,64,128]{4,3,2,1,0:T(8,128)(2,1)S(1)}, bf16[4,3,2,64,128]{4,3,2,1,0:T(8,128)(2,1)S(1)}, u32[]{:S(2)}, u32[]{:S(2)}) %collective-permute-start.21) | collective-permute-done | bytes 393248 | tf_op jit(solution)/shard_map/ppermute | solution.py:28
  65.7 0.6 collective-permute-start.22
  66.3 2.7 %collective-permute-start.20 = (bf16[4,3,2,64,128]{4,3,2,1,0:T(8,128)(2,1)S(1)}, bf16[4,3,2,64,128]{4,3,2,1,0:T(8,128)(2,1)S(1)}, u32[]{:S(2)}, u32[]{:S(2)}) collective-permute-start(bf16[4,3,2,64,128]{4,3,2,1,0:T(8,128)(2,1)S(1)} %collective-permute-done.19.refs_14_), channel_id=1, source_target_pairs={{0,1},{1,0},{2,3},{3,2},{4,5},{5,4},{6,7},{7,6},{8,9},{9,8},{10,11... | collective-permute-start | bytes 1179656 | tf_op jit(solution)/shard_map/ppermute | solution.py:28
  69.0 1.3 %collective-permute-done.20.refs_15_ = bf16[4,3,2,64,128]{4,3,2,1,0:T(8,128)(2,1)S(1)} collective-permute-done((bf16[4,3,2,64,128]{4,3,2,1,0:T(8,128)(2,1)S(1)}, bf16[4,3,2,64,128]{4,3,2,1,0:T(8,128)(2,1)S(1)}, u32[]{:S(2)}, u32[]{:S(2)}) %collective-permute-start.20) | collective-permute-done | bytes 393248 | tf_op jit(solution)/shard_map/ppermute | solution.py:28
  70.3 4.3 %levels.1 = (bf16[16,64,128]{2,1,0:T(8,128)(2,1)S(1)}, bf16[16,64,128]{2,1,0:T(8,128)(2,1)S(1)}, bf16[16,64,128]{2,1,0:T(8,128)(2,1)S(1)}, bf16[16,64,128]{2,1,0...) custom-call(bf16[16,64,128]{2,1,0:T(8,128)(2,1)S(1)} %get-tuple-elem, ...), custom_call_target="tpu_custom_call" | custom-call | tf_op jit(solution)/shard_map/levels/pallas_call | solution.py:181
  74.6 1.7 %collective-permute-start.28 = (bf16[16,64,128]{2,1,0:T(8,128)(2,1)S(1)}, bf16[16,64,128]{2,1,0:T(8,128)(2,1)S(1)}, u32[]{:S(2)}, u32[]{:S(2)}) collective-permute-start(bf16[16,64,128]{2,1,0:T(8,128)(2,1)S(1)} %get-tuple-element.34), channel_id=1, source_target_pairs={{0,48},{1,49},{2,50},{3,51},{4,52},{5,53},{6,54},{7,55},{8,56},{9,... | collective-permute-start | bytes 786440 | tf_op jit(solution)/shard_map/ppermute | solution.py:28
  76.3 2.1 %collective-permute-start.29 = (bf16[16,64,128]{2,1,0:T(8,128)(2,1)S(1)}, bf16[16,64,128]{2,1,0:T(8,128)(2,1)S(1)}, u32[]{:S(2)}, u32[]{:S(2)}) collective-permute-start(bf16[16,64,128]{2,1,0:T(8,128)(2,1)S(1)} %get-tuple-element.35), channel_id=1, source_target_pairs={{0,56},{1,57},{2,58},{3,59},{4,60},{5,61},{6,62},{7,63},{8,48},{9,... | collective-permute-start | bytes 786440 | tf_op jit(solution)/shard_map/ppermute | solution.py:28
  78.4 1.0 collective-permute-start.25
  79.4 1.1 %collective-permute-start.27 = (bf16[16,64,128]{2,1,0:T(8,128)(2,1)}, bf16[16,64,128]{2,1,0:T(8,128)(2,1)S(1)}, u32[]{:S(2)}, u32[]{:S(2)}) collective-permute-start(bf16[16,64,128]{2,1,0:T(8,128)(2,1)} %get-tuple-element.33), channel_id=1, source_target_pairs={{0,40},{1,41},{2,42},{3,43},{4,44},{5,45},{6,46},{7,47},{8,32},{9,... | collective-permute-start | bytes 786440 | tf_op jit(solution)/shard_map/ppermute | solution.py:28
  80.5 0.6 collective-permute-start.26
  81.1 3.4 %collective-permute-done.28.refs_1_ = bf16[16,64,128]{2,1,0:T(8,128)(2,1)S(1)} collective-permute-done((bf16[16,64,128]{2,1,0:T(8,128)(2,1)S(1)}, bf16[16,64,128]{2,1,0:T(8,128)(2,1)S(1)}, u32[]{:S(2)}, u32[]{:S(2)}) %collective-permute-start.28) | collective-permute-done | bytes 262176 | tf_op jit(solution)/shard_map/ppermute | solution.py:28
  84.5 1.6 %collective-permute-start.24 = (bf16[16,64,128]{2,1,0:T(8,128)(2,1)S(1)}, bf16[16,64,128]{2,1,0:T(8,128)(2,1)S(1)}, u32[]{:S(2)}, u32[]{:S(2)}) collective-permute-start(bf16[16,64,128]{2,1,0:T(8,128)(2,1)S(1)} %get-tuple-element.30), channel_id=1, source_target_pairs={{0,24},{1,25},{2,26},{3,27},{4,28},{5,29},{6,30},{7,31},{8,16},{9,... | collective-permute-start | bytes 786440 | tf_op jit(solution)/shard_map/ppermute | solution.py:28
  86.1 8.3 %collective-permute-done.29.refs_1_ = bf16[16,64,128]{2,1,0:T(8,128)(2,1)S(1)} collective-permute-done((bf16[16,64,128]{2,1,0:T(8,128)(2,1)S(1)}, bf16[16,64,128]{2,1,0:T(8,128)(2,1)S(1)}, u32[]{:S(2)}, u32[]{:S(2)}) %collective-permute-start.29) | collective-permute-done | bytes 262176 | tf_op jit(solution)/shard_map/ppermute | solution.py:28
  94.4 0.1 copy.21.refs_3_
  94.6 1.8 %interp_out.8.refs_4_ = bf16[8,8,2,160,128]{4,3,2,1,0:T(8,128)(2,1)} custom-call(s32[2]{0:T(128)S(1)} %pad_add_fusion.refs_0_, bf16[16,64,128]{2,1,0:T(8,128)(2,1)S(1)} %get-tuple-element.36.refs_1_, f32[160,128]{1,0:T(8,128)S(1)} %bitcast.23, bf16[160,64]{1,0:T(8,128)(2,1)S(1)} %copy.21.refs_3_), custom_call_target="tpu_custom_call" | custom-call | tf_op jit(solution)/shard_map/interp_out/pallas_call | solution.py:125
  96.3 1.8 %interp_out.9.refs_4_ = bf16[8,8,2,160,128]{4,3,2,1,0:T(8,128)(2,1)} custom-call(s32[2]{0:T(128)S(1)} %pad_add_fusion.refs_0_, bf16[16,64,128]{2,1,0:T(8,128)(2,1)S(1)} %collective-permute-done.29.refs_1_, f32[160,128]{1,0:T(8,128)S(1)} %bitcast.24, bf16[160,64]{1,0:T(8,128)(2,1)S(1)} %copy.21.refs_3_, ...), custom_call_target="tpu_custom_call", output_to_operand_aliasing={{}: (4, {})} | custom-call | tf_op jit(solution)/shard_map/interp_out/pallas_call | solution.py:125
  98.1 1.8 %interp_out.10.refs_4_ = bf16[8,8,2,160,128]{4,3,2,1,0:T(8,128)(2,1)} custom-call(s32[2]{0:T(128)S(1)} %pad_add_fusion.refs_0_, bf16[16,64,128]{2,1,0:T(8,128)(2,1)S(1)} %collective-permute-done.28.refs_1_, f32[160,128]{1,0:T(8,128)S(1)} %bitcast.25, bf16[160,64]{1,0:T(8,128)(2,1)S(1)} %copy.21.refs_3_, ...), custom_call_target="tpu_custom_call", output_to_operand_aliasing={{}: (4, {})} | custom-call | tf_op jit(solution)/shard_map/interp_out/pallas_call | solution.py:125
  99.9 1.8 %interp_out.11.refs_4_ = bf16[8,8,2,160,128]{4,3,2,1,0:T(8,128)(2,1)} custom-call(s32[2]{0:T(128)S(1)} %pad_add_fusion.refs_0_, bf16[16,64,128]{2,1,0:T(8,128)(2,1)S(1)} %collective-permute-done.27.refs_1_, f32[160,128]{1,0:T(8,128)S(1)} %bitcast.26, bf16[160,64]{1,0:T(8,128)(2,1)S(1)} %copy.21.refs_3_, ...), custom_call_target="tpu_custom_call", output_to_operand_aliasing={{}: (4, {})} | custom-call | tf_op jit(solution)/shard_map/interp_out/pallas_call | solution.py:125
  101.7 1.9 %collective-permute-done.26.refs_1_ = bf16[16,64,128]{2,1,0:T(8,128)(2,1)S(1)} collective-permute-done((bf16[16,64,128]{2,1,0:T(8,128)(2,1)}, bf16[16,64,128]{2,1,0:T(8,128)(2,1)S(1)}, u32[]{:S(2)}, u32[]{:S(2)}) %collective-permute-start.26) | collective-permute-done | bytes 262176 | tf_op jit(solution)/shard_map/ppermute | solution.py:28
  103.6 1.8 %interp_out.12.refs_4_ = bf16[8,8,2,160,128]{4,3,2,1,0:T(8,128)(2,1)} custom-call(s32[2]{0:T(128)S(1)} %pad_add_fusion.refs_0_, bf16[16,64,128]{2,1,0:T(8,128)(2,1)S(1)} %collective-permute-done.26.refs_1_, f32[160,128]{1,0:T(8,128)S(1)} %bitcast.27, bf16[160,64]{1,0:T(8,128)(2,1)S(1)} %copy.21.refs_3_, ...), custom_call_target="tpu_custom_call", output_to_operand_aliasing={{}: (4, {})} | custom-call | tf_op jit(solution)/shard_map/interp_out/pallas_call | solution.py:125
  105.4 1.8 %interp_out.13.refs_4_ = bf16[8,8,2,160,128]{4,3,2,1,0:T(8,128)(2,1)} custom-call(s32[2]{0:T(128)S(1)} %pad_add_fusion.refs_0_, bf16[16,64,128]{2,1,0:T(8,128)(2,1)S(1)} %collective-permute-done.25.refs_1_, f32[160,128]{1,0:T(8,128)S(1)} %bitcast.28, bf16[160,64]{1,0:T(8,128)(2,1)S(1)} %copy.21.refs_3_, ...), custom_call_target="tpu_custom_call", output_to_operand_aliasing={{}: (4, {})} | custom-call | tf_op jit(solution)/shard_map/interp_out/pallas_call | solution.py:125
  107.1 1.8 %interp_out.14.refs_4_ = bf16[8,8,2,160,128]{4,3,2,1,0:T(8,128)(2,1)} custom-call(s32[2]{0:T(128)S(1)} %pad_add_fusion.refs_0_, bf16[16,64,128]{2,1,0:T(8,128)(2,1)S(1)} %collective-permute-done.24.refs_1_, f32[160,128]{1,0:T(8,128)S(1)} %bitcast.29, bf16[160,64]{1,0:T(8,128)(2,1)S(1)} %copy.21.refs_3_, ...), custom_call_target="tpu_custom_call", output_to_operand_aliasing={{}: (4, {})} | custom-call | tf_op jit(solution)/shard_map/interp_out/pallas_call | solution.py:125
  108.9 1.8 %interp_out.15 = bf16[8,8,2,160,128]{4,3,2,1,0:T(8,128)(2,1)} custom-call(s32[2]{0:T(128)S(1)} %pad_add_fusion.refs_0_, bf16[16,64,128]{2,1,0:T(8,128)(2,1)S(1)} %collective-permute-done.23.refs_1_, f32[160,128]{1,0:T(8,128)S(1)} %bitcast.30, bf16[160,64]{1,0:T(8,128)(2,1)S(1)} %copy.21.refs_3_, ...), custom_call_target="tpu_custom_call", output_to_operand_aliasing={{}: (4, {})} | custom-call | tf_op jit(solution)/shard_map/interp_out/pallas_call | solution.py:125
  (40 shorter events, 0.4 us)
Async XLA Ops:
  1.2 22.1 %collective-permute-start.13 = (bf16[3,2,64,128]{3,2,1,0:T(8,128)(2,1)S(1)}, bf16[3,2,64,128]{3,2,1,0:T(8,128)(2,1)S(1)}, u32[]{:S(2)}, u32[]{:S(2)}) collective-permute-start(bf16[3,2,64,128]{3,2,1,0:T(8,128)(2,1)S(1)} %get-tuple-element.37), channel_id=1, source_target_pairs={{0,56},{1,57},{2,58},{3,59},{4,60},{5,61},{6,62},{7,63},{8,48},{9,... | collective-permute-start | bytes 294920 | tf_op jit(solution)/shard_map/ppermute | solution.py:28
  6.0 14.0 %collective-permute-start.11 = (bf16[3,2,64,128]{3,2,1,0:T(8,128)(2,1)S(1)}, bf16[3,2,64,128]{3,2,1,0:T(8,128)(2,1)S(1)}, u32[]{:S(2)}, u32[]{:S(2)}) collective-permute-start(bf16[3,2,64,128]{3,2,1,0:T(8,128)(2,1)S(1)} %get-tuple-element.38), channel_id=1, source_target_pairs={{0,40},{1,41},{2,42},{3,43},{4,44},{5,45},{6,46},{7,47},{8,32},{9,... | collective-permute-start | bytes 294920 | tf_op jit(solution)/shard_map/ppermute | solution.py:28
  6.0 13.9 %collective-permute-start.10 = (bf16[3,2,64,128]{3,2,1,0:T(8,128)(2,1)S(1)}, bf16[3,2,64,128]{3,2,1,0:T(8,128)(2,1)S(1)}, u32[]{:S(2)}, u32[]{:S(2)}) collective-permute-start(bf16[3,2,64,128]{3,2,1,0:T(8,128)(2,1)S(1)} %get-tuple-element.39), channel_id=1, source_target_pairs={{0,32},{1,33},{2,34},{3,35},{4,36},{5,37},{6,38},{7,39},{8,40},{9,... | collective-permute-start | bytes 294920 | tf_op jit(solution)/shard_map/ppermute | solution.py:28
  7.1 12.8 %collective-permute-start.9 = (bf16[3,2,64,128]{3,2,1,0:T(8,128)(2,1)S(1)}, bf16[3,2,64,128]{3,2,1,0:T(8,128)(2,1)S(1)}, u32[]{:S(2)}, u32[]{:S(2)}) collective-permute-start(bf16[3,2,64,128]{3,2,1,0:T(8,128)(2,1)S(1)} %get-tuple-element.40), channel_id=1, source_target_pairs={{0,24},{1,25},{2,26},{3,27},{4,28},{5,29},{6,30},{7,31},{8,16},{9,... | collective-permute-start | bytes 294920 | tf_op jit(solution)/shard_map/ppermute | solution.py:28
  8.0 4.5 %collective-permute-start.7 = (bf16[3,2,64,128]{3,2,1,0:T(8,128)(2,1)S(1)}, bf16[3,2,64,128]{3,2,1,0:T(8,128)(2,1)S(1)}, u32[]{:S(2)}, u32[]{:S(2)}) collective-permute-start(bf16[3,2,64,128]{3,2,1,0:T(8,128)(2,1)S(1)} %get-tuple-element.42), channel_id=1, source_target_pairs={{0,8},{1,9},{2,10},{3,11},{4,12},{5,13},{6,14},{7,15},{8,0},{9,1},... | collective-permute-start | bytes 294920 | tf_op jit(solution)/shard_map/ppermute | solution.py:28
  12.4 5.0 %collective-permute-start.8 = (bf16[3,2,64,128]{3,2,1,0:T(8,128)(2,1)S(1)}, bf16[3,2,64,128]{3,2,1,0:T(8,128)(2,1)S(1)}, u32[]{:S(2)}, u32[]{:S(2)}) collective-permute-start(bf16[3,2,64,128]{3,2,1,0:T(8,128)(2,1)S(1)} %get-tuple-element.41), channel_id=1, source_target_pairs={{0,16},{1,17},{2,18},{3,19},{4,20},{5,21},{6,22},{7,23},{8,24},{9,... | collective-permute-start | bytes 294920 | tf_op jit(solution)/shard_map/ppermute | solution.py:28
  17.4 5.9 %collective-permute-start.12 = (bf16[3,2,64,128]{3,2,1,0:T(8,128)(2,1)S(1)}, bf16[3,2,64,128]{3,2,1,0:T(8,128)(2,1)S(1)}, u32[]{:S(2)}, u32[]{:S(2)}) collective-permute-start(bf16[3,2,64,128]{3,2,1,0:T(8,128)(2,1)S(1)} %get-tuple-element.43), channel_id=1, source_target_pairs={{0,48},{1,49},{2,50},{3,51},{4,52},{5,53},{6,54},{7,55},{8,56},{9,... | collective-permute-start | bytes 294920 | tf_op jit(solution)/shard_map/ppermute | solution.py:28
  23.3 18.8 %collective-permute-start.17 = (bf16[8,3,2,64,128]{4,3,2,1,0:T(8,128)(2,1)S(1)}, bf16[8,3,2,64,128]{4,3,2,1,0:T(8,128)(2,1)S(1)}, u32[]{:S(2)}, u32[]{:S(2)}) collective-permute-start(bf16[8,3,2,64,128]{4,3,2,1,0:T(8,128)(2,1)S(1)} %bitcast_dynamic-update-slice_fusion.refs_8_), channel_id=1, source_target_pairs={{0,6},{1,7},{2,4},{3,5},{4,2},{5,3},{6,0},{7,1},{8,14},{9,15},{10,... | collective-permute-start | bytes 2359304 | tf_op jit(solution)/shard_map/ppermute | solution.py:28
  26.1 16.0 %collective-permute-start.15 = (bf16[8,3,2,64,128]{4,3,2,1,0:T(8,128)(2,1)S(1)}, bf16[8,3,2,64,128]{4,3,2,1,0:T(8,128)(2,1)S(1)}, u32[]{:S(2)}, u32[]{:S(2)}) collective-permute-start(bf16[8,3,2,64,128]{4,3,2,1,0:T(8,128)(2,1)S(1)} %bitcast_dynamic-update-slice_fusion.refs_8_), channel_id=1, source_target_pairs={{0,2},{1,3},{2,0},{3,1},{4,6},{5,7},{6,4},{7,5},{8,10},{9,11},{10,... | collective-permute-start | bytes 2359304 | tf_op jit(solution)/shard_map/ppermute | solution.py:28
  29.0 8.3 %collective-permute-start.4 = (bf16[16,64,128]{2,1,0:T(8,128)(2,1)S(1)}, bf16[16,64,128]{2,1,0:T(8,128)(2,1)S(1)}, u32[]{:S(2)}, u32[]{:S(2)}) collective-permute-start(bf16[16,64,128]{2,1,0:T(8,128)(2,1)S(1)} %get-tuple-element.26), channel_id=1, source_target_pairs={{0,40},{1,41},{2,42},{3,43},{4,44},{5,45},{6,46},{7,47},{8,32},{9,... | collective-permute-start | bytes 786440 | tf_op jit(solution)/shard_map/ppermute | solution.py:28
  29.8 9.8 %collective-permute-start.5 = (bf16[16,64,128]{2,1,0:T(8,128)(2,1)S(1)}, bf16[16,64,128]{2,1,0:T(8,128)(2,1)S(1)}, u32[]{:S(2)}, u32[]{:S(2)}) collective-permute-start(bf16[16,64,128]{2,1,0:T(8,128)(2,1)S(1)} %get-tuple-element.27), channel_id=1, source_target_pairs={{0,48},{1,49},{2,50},{3,51},{4,52},{5,53},{6,54},{7,55},{8,56},{9,... | collective-permute-start | bytes 786440 | tf_op jit(solution)/shard_map/ppermute | solution.py:28
  32.7 11.8 %collective-permute-start.6 = (bf16[16,64,128]{2,1,0:T(8,128)(2,1)S(1)}, bf16[16,64,128]{2,1,0:T(8,128)(2,1)S(1)}, u32[]{:S(2)}, u32[]{:S(2)}) collective-permute-start(bf16[16,64,128]{2,1,0:T(8,128)(2,1)S(1)} %get-tuple-element.28), channel_id=1, source_target_pairs={{0,56},{1,57},{2,58},{3,59},{4,60},{5,61},{6,62},{7,63},{8,48},{9,... | collective-permute-start | bytes 786440 | tf_op jit(solution)/shard_map/ppermute | solution.py:28
  37.3 57.1 %copy-start.1 = (bf16[160,64]{0,1:T(8,128)(2,1)S(1)}, bf16[160,64]{0,1:T(8,128)(2,1)}, u32[]{:S(2)}) copy-start(bf16[160,64]{0,1:T(8,128)(2,1)} %param.10) | copy-start | bytes 61444
  37.3 57.2 %copy-start = (f32[128,160]{0,1:T(8,128)S(1)}, f32[128,160]{0,1:T(8,128)}, u32[]{:S(2)}) copy-start(f32[128,160]{0,1:T(8,128)} %param.11) | copy-start | bytes 245764
  37.3 17.1 %collective-permute-start = (bf16[16,64,128]{2,1,0:T(8,128)(2,1)S(1)}, bf16[16,64,128]{2,1,0:T(8,128)(2,1)S(1)}, u32[]{:S(2)}, u32[]{:S(2)}) collective-permute-start(bf16[16,64,128]{2,1,0:T(8,128)(2,1)S(1)} %get-tuple-element.22), channel_id=1, source_target_pairs={{0,8},{1,9},{2,10},{3,11},{4,12},{5,13},{6,14},{7,15},{8,0},{9,1},... | collective-permute-start | bytes 786440 | tf_op jit(solution)/shard_map/ppermute | solution.py:28
  39.6 16.6 %collective-permute-start.1 = (bf16[16,64,128]{2,1,0:T(8,128)(2,1)S(1)}, bf16[16,64,128]{2,1,0:T(8,128)(2,1)S(1)}, u32[]{:S(2)}, u32[]{:S(2)}) collective-permute-start(bf16[16,64,128]{2,1,0:T(8,128)(2,1)S(1)} %get-tuple-element.23), channel_id=1, source_target_pairs={{0,16},{1,17},{2,18},{3,19},{4,20},{5,21},{6,22},{7,23},{8,24},{9,... | collective-permute-start | bytes 786440 | tf_op jit(solution)/shard_map/ppermute | solution.py:28
  42.1 17.8 %collective-permute-start.2 = (bf16[16,64,128]{2,1,0:T(8,128)(2,1)S(1)}, bf16[16,64,128]{2,1,0:T(8,128)(2,1)S(1)}, u32[]{:S(2)}, u32[]{:S(2)}) collective-permute-start(bf16[16,64,128]{2,1,0:T(8,128)(2,1)S(1)} %get-tuple-element.24), channel_id=1, source_target_pairs={{0,24},{1,25},{2,26},{3,27},{4,28},{5,29},{6,30},{7,31},{8,16},{9,... | collective-permute-start | bytes 786440 | tf_op jit(solution)/shard_map/ppermute | solution.py:28
  42.2 20.4 %collective-permute-start.3 = (bf16[16,64,128]{2,1,0:T(8,128)(2,1)S(1)}, bf16[16,64,128]{2,1,0:T(8,128)(2,1)S(1)}, u32[]{:S(2)}, u32[]{:S(2)}) collective-permute-start(bf16[16,64,128]{2,1,0:T(8,128)(2,1)S(1)} %get-tuple-element.25), channel_id=1, source_target_pairs={{0,32},{1,33},{2,34},{3,35},{4,36},{5,37},{6,38},{7,39},{8,40},{9,... | collective-permute-start | bytes 786440 | tf_op jit(solution)/shard_map/ppermute | solution.py:28
  44.4 24.5 %collective-permute-start.14 = (bf16[8,3,2,64,128]{4,3,2,1,0:T(8,128)(2,1)S(1)}, bf16[8,3,2,64,128]{4,3,2,1,0:T(8,128)(2,1)S(1)}, u32[]{:S(2)}, u32[]{:S(2)}) collective-permute-start(bf16[8,3,2,64,128]{4,3,2,1,0:T(8,128)(2,1)S(1)} %bitcast_dynamic-update-slice_fusion.refs_8_), channel_id=1, source_target_pairs={{0,1},{1,0},{2,3},{3,2},{4,5},{5,4},{6,7},{7,6},{8,9},{9,8},{10,11... | collective-permute-start | bytes 2359304 | tf_op jit(solution)/shard_map/ppermute | solution.py:28
  54.4 11.3 %collective-permute-start.21 = (bf16[4,3,2,64,128]{4,3,2,1,0:T(8,128)(2,1)S(1)}, bf16[4,3,2,64,128]{4,3,2,1,0:T(8,128)(2,1)S(1)}, u32[]{:S(2)}, u32[]{:S(2)}) collective-permute-start(bf16[4,3,2,64,128]{4,3,2,1,0:T(8,128)(2,1)S(1)} %slice.9), channel_id=1, source_target_pairs={{0,2},{1,3},{2,0},{3,1},{4,6},{5,7},{6,4},{7,5},{8,10},{9,11},{10,... | collective-permute-start | bytes 1179656 | tf_op jit(solution)/shard_map/ppermute | solution.py:28
  56.2 10.1 %collective-permute-start.19 = (bf16[4,3,2,64,128]{4,3,2,1,0:T(8,128)(2,1)S(1)}, bf16[4,3,2,64,128]{4,3,2,1,0:T(8,128)(2,1)S(1)}, u32[]{:S(2)}, u32[]{:S(2)}) collective-permute-start(bf16[4,3,2,64,128]{4,3,2,1,0:T(8,128)(2,1)S(1)} %slice.8), channel_id=1, source_target_pairs={{0,6},{1,7},{2,4},{3,5},{4,2},{5,3},{6,0},{7,1},{8,14},{9,15},{10,... | collective-permute-start | bytes 1179656 | tf_op jit(solution)/shard_map/ppermute | solution.py:28
  59.9 9.0 %collective-permute-start.18 = (bf16[8,3,2,64,128]{4,3,2,1,0:T(8,128)(2,1)S(1)}, bf16[8,3,2,64,128]{4,3,2,1,0:T(8,128)(2,1)S(1)}, u32[]{:S(2)}, u32[]{:S(2)}) collective-permute-start(bf16[8,3,2,64,128]{4,3,2,1,0:T(8,128)(2,1)S(1)} %collective-permute-done.17.refs_12_), channel_id=1, source_target_pairs={{0,1},{1,0},{2,3},{3,2},{4,5},{5,4},{6,7},{7,6},{8,9},{9,8},{10,11... | collective-permute-start | bytes 2359304 | tf_op jit(solution)/shard_map/ppermute | solution.py:28
  62.5 7.8 %collective-permute-start.16 = (bf16[8,3,2,64,128]{4,3,2,1,0:T(8,128)(2,1)S(1)}, bf16[8,3,2,64,128]{4,3,2,1,0:T(8,128)(2,1)S(1)}, u32[]{:S(2)}, u32[]{:S(2)}) collective-permute-start(bf16[8,3,2,64,128]{4,3,2,1,0:T(8,128)(2,1)S(1)} %collective-permute-done.15.refs_10_), channel_id=1, source_target_pairs={{0,1},{1,0},{2,3},{3,2},{4,5},{5,4},{6,7},{7,6},{8,9},{9,8},{10,11... | collective-permute-start | bytes 2359304 | tf_op jit(solution)/shard_map/ppermute | solution.py:28
  65.7 3.3 %collective-permute-start.22 = (bf16[4,3,2,64,128]{4,3,2,1,0:T(8,128)(2,1)S(1)}, bf16[4,3,2,64,128]{4,3,2,1,0:T(8,128)(2,1)S(1)}, u32[]{:S(2)}, u32[]{:S(2)}) collective-permute-start(bf16[4,3,2,64,128]{4,3,2,1,0:T(8,128)(2,1)S(1)} %collective-permute-done.21.refs_16_), channel_id=1, source_target_pairs={{0,1},{1,0},{2,3},{3,2},{4,5},{5,4},{6,7},{7,6},{8,9},{9,8},{10,11... | collective-permute-start | bytes 1179656 | tf_op jit(solution)/shard_map/ppermute | solution.py:28
  66.3 4.0 %collective-permute-start.20 = (bf16[4,3,2,64,128]{4,3,2,1,0:T(8,128)(2,1)S(1)}, bf16[4,3,2,64,128]{4,3,2,1,0:T(8,128)(2,1)S(1)}, u32[]{:S(2)}, u32[]{:S(2)}) collective-permute-start(bf16[4,3,2,64,128]{4,3,2,1,0:T(8,128)(2,1)S(1)} %collective-permute-done.19.refs_14_), channel_id=1, source_target_pairs={{0,1},{1,0},{2,3},{3,2},{4,5},{5,4},{6,7},{7,6},{8,9},{9,8},{10,11... | collective-permute-start | bytes 1179656 | tf_op jit(solution)/shard_map/ppermute | solution.py:28
  74.6 9.9 %collective-permute-start.28 = (bf16[16,64,128]{2,1,0:T(8,128)(2,1)S(1)}, bf16[16,64,128]{2,1,0:T(8,128)(2,1)S(1)}, u32[]{:S(2)}, u32[]{:S(2)}) collective-permute-start(bf16[16,64,128]{2,1,0:T(8,128)(2,1)S(1)} %get-tuple-element.34), channel_id=1, source_target_pairs={{0,48},{1,49},{2,50},{3,51},{4,52},{5,53},{6,54},{7,55},{8,56},{9,... | collective-permute-start | bytes 786440 | tf_op jit(solution)/shard_map/ppermute | solution.py:28
  76.3 18.1 %collective-permute-start.29 = (bf16[16,64,128]{2,1,0:T(8,128)(2,1)S(1)}, bf16[16,64,128]{2,1,0:T(8,128)(2,1)S(1)}, u32[]{:S(2)}, u32[]{:S(2)}) collective-permute-start(bf16[16,64,128]{2,1,0:T(8,128)(2,1)S(1)} %get-tuple-element.35), channel_id=1, source_target_pairs={{0,56},{1,57},{2,58},{3,59},{4,60},{5,61},{6,62},{7,63},{8,48},{9,... | collective-permute-start | bytes 786440 | tf_op jit(solution)/shard_map/ppermute | solution.py:28
  78.4 27.0 %collective-permute-start.25 = (bf16[16,64,128]{2,1,0:T(8,128)(2,1)S(1)}, bf16[16,64,128]{2,1,0:T(8,128)(2,1)S(1)}, u32[]{:S(2)}, u32[]{:S(2)}) collective-permute-start(bf16[16,64,128]{2,1,0:T(8,128)(2,1)S(1)} %get-tuple-element.31), channel_id=1, source_target_pairs={{0,16},{1,17},{2,18},{3,19},{4,20},{5,21},{6,22},{7,23},{8,24},{9,... | collective-permute-start | bytes 786440 | tf_op jit(solution)/shard_map/ppermute | solution.py:28
  79.4 20.6 %collective-permute-start.27 = (bf16[16,64,128]{2,1,0:T(8,128)(2,1)}, bf16[16,64,128]{2,1,0:T(8,128)(2,1)S(1)}, u32[]{:S(2)}, u32[]{:S(2)}) collective-permute-start(bf16[16,64,128]{2,1,0:T(8,128)(2,1)} %get-tuple-element.33), channel_id=1, source_target_pairs={{0,40},{1,41},{2,42},{3,43},{4,44},{5,45},{6,46},{7,47},{8,32},{9,... | collective-permute-start | bytes 786440 | tf_op jit(solution)/shard_map/ppermute | solution.py:28
  80.5 23.1 %collective-permute-start.26 = (bf16[16,64,128]{2,1,0:T(8,128)(2,1)}, bf16[16,64,128]{2,1,0:T(8,128)(2,1)S(1)}, u32[]{:S(2)}, u32[]{:S(2)}) collective-permute-start(bf16[16,64,128]{2,1,0:T(8,128)(2,1)} %get-tuple-element.32), channel_id=1, source_target_pairs={{0,32},{1,33},{2,34},{3,35},{4,36},{5,37},{6,38},{7,39},{8,40},{9,... | collective-permute-start | bytes 786440 | tf_op jit(solution)/shard_map/ppermute | solution.py:28
  84.5 22.6 %collective-permute-start.24 = (bf16[16,64,128]{2,1,0:T(8,128)(2,1)S(1)}, bf16[16,64,128]{2,1,0:T(8,128)(2,1)S(1)}, u32[]{:S(2)}, u32[]{:S(2)}) collective-permute-start(bf16[16,64,128]{2,1,0:T(8,128)(2,1)S(1)} %get-tuple-element.30), channel_id=1, source_target_pairs={{0,24},{1,25},{2,26},{3,27},{4,28},{5,29},{6,30},{7,31},{8,16},{9,... | collective-permute-start | bytes 786440 | tf_op jit(solution)/shard_map/ppermute | solution.py:28
  94.4 14.5 %collective-permute-start.23 = (bf16[16,64,128]{2,1,0:T(8,128)(2,1)S(1)}, bf16[16,64,128]{2,1,0:T(8,128)(2,1)S(1)}, u32[]{:S(2)}, u32[]{:S(2)}) collective-permute-start(bf16[16,64,128]{2,1,0:T(8,128)(2,1)S(1)} %get-tuple-element.29), channel_id=1, source_target_pairs={{0,8},{1,9},{2,10},{3,11},{4,12},{5,13},{6,14},{7,15},{8,0},{9,1},... | collective-permute-start | bytes 786440 | tf_op jit(solution)/shard_map/ppermute | solution.py:28
